TPU v7x, 256 devices: a whole 4x4x8 slice. The times are simulated.
256 devices in a mesh: frame: 16 (over z_hi, y), space: 16 (over z_lo, x, core).
Axes of the slice: x: 4, y: 4, z: 8 (z_hi: 4, z_lo: 2; z = z_hi * 2 + z_lo), core: 2. Of those that a mesh axis runs over, the one named last changes fastest.
Arguments:
- hidden_in: bfloat16 [2, 16, 32, 64, 1152], P(None, 'frame', 'space'), may hold values from -6 to 6
- attn_cotangent: bfloat16 [2, 16, 32, 64, 1152], P(None, 'frame', 'space'), may hold values from -6 to 6
- w_qkv: bfloat16 [1152, 3456], P('space'), may hold values from -0.1875 to 0.1875
- modulation_table: bfloat16 [1000, 2, 1152], replicated, may hold values from -3 to 3
- snr_table: float32 [1000], replicated, may hold values from 0.1 to 1
- timestep: int32 [2], replicated, may hold values from 0 to 999
- weight_index: int32 [2], replicated, may hold values from 0 to 999
Outputs:
- grad_input: bfloat16 [2, 16, 32, 64, 1152], P(None, 'frame', 'space')
- grad_w_qkv: float32 [1152, 3456], P('space')
- grad_modulation: float32 [2, 2, 1152], replicated
All inputs are finite; a program needn't handle non-finite values.
Results may differ from a plain program's by a relative error of at most 0.029.
Values may be sent and summed in bfloat16 or wider, within the bound.
A program may use at most 128 MiB of HBM per device.

v0:
```python
import jax
import jax.numpy as jnp
from jax import lax
from jax.sharding import PartitionSpec as P

HEADS = 16
HEAD_DIM = 72


def attend_back(queries, keys, values, upstream):
    factor = queries.shape[-1] ** (-0.5)
    queries = queries.astype(jnp.float32)
    keys = keys.astype(jnp.float32)
    values = values.astype(jnp.float32)
    upstream = upstream.astype(jnp.float32)
    highest = lax.Precision.HIGHEST
    scores = jnp.einsum("bfxhe,bgxhe->bxhfg", queries, keys, precision=highest) * factor
    expd = jnp.exp(scores)
    probs = expd / jnp.sum(expd, axis=-1, keepdims=True)
    grad_probs = jnp.einsum("bfxhe,bgxhe->bxhfg", upstream, values, precision=highest)
    grad_values = jnp.einsum("bxhfg,bfxhe->bgxhe", probs, upstream, precision=highest)
    grad_scores = probs * (grad_probs - jnp.sum(probs * grad_probs, axis=-1, keepdims=True))
    grad_queries = jnp.einsum("bxhfg,bgxhe->bfxhe", grad_scores, keys, precision=highest) * factor
    grad_keys = jnp.einsum("bxhfg,bfxhe->bgxhe", grad_scores, queries, precision=highest) * factor
    return (
        grad_queries.astype(jnp.bfloat16),
        grad_keys.astype(jnp.bfloat16),
        grad_values.astype(jnp.bfloat16),
    )


def per_device(
    hidden_in, attn_cotangent, w_qkv, modulation_table, snr_table, timestep, weight_index
):
    clip_count, frame_dev, row_dev, col_count, model_width = hidden_in.shape
    positions = row_dev * col_count
    values_in = hidden_in.astype(jnp.float32)
    average = jnp.mean(values_in, axis=-1, keepdims=True)
    centered = values_in - average
    variance = jnp.mean(centered * centered, axis=-1, keepdims=True)
    inverse_std = lax.rsqrt(variance + 1e-06)
    normed = centered * inverse_std
    modulation = modulation_table[timestep].astype(jnp.float32)
    shift = modulation[:, 0][:, None, None, None, :]
    scale = modulation[:, 1][:, None, None, None, :]
    modulated = (normed * (1.0 + scale) + shift).astype(jnp.bfloat16)
    mod_rows = modulated.reshape(-1, model_width)
    w_full = lax.all_gather(w_qkv, "space", axis=0, tiled=True)
    projected = jnp.dot(mod_rows, w_full, preferred_element_type=jnp.float32).astype(jnp.bfloat16)
    projected = projected.reshape(clip_count, frame_dev, positions, 3, model_width)
    loss_weight = snr_table[weight_index]
    upstream = (loss_weight[:, None, None, None, None] * attn_cotangent.astype(jnp.float32)).astype(
        jnp.bfloat16
    )
    upstream = upstream.reshape(clip_count, frame_dev, positions, 1, model_width)
    packed = jnp.concatenate([projected, upstream], axis=3)
    received = lax.all_to_all(packed, "frame", split_axis=2, concat_axis=1, tiled=True)
    item_count = received.shape[0]
    frames = received.shape[1]
    across = received.shape[2]
    pieces = received.reshape(item_count, frames, across, 4, HEADS, HEAD_DIM)
    head_grads = attend_back(
        pieces[:, :, :, 0], pieces[:, :, :, 1], pieces[:, :, :, 2], pieces[:, :, :, 3]
    )
    stacked = jnp.stack(head_grads, axis=3).reshape(item_count, frames, across, 3, model_width)
    grad_projected = lax.all_to_all(stacked, "frame", split_axis=1, concat_axis=2, tiled=True)
    grad_rows = grad_projected.reshape(-1, 3 * model_width)
    device_count = lax.axis_size("frame") * lax.axis_size("space")
    grad_scale_factor = float(mod_rows.shape[0] * device_count) ** (-0.5)
    row_share = lax.psum_scatter(
        lax.dot_general(
            mod_rows, grad_rows, (((0,), (0,)), ((), ())), preferred_element_type=jnp.float32
        ).astype(jnp.bfloat16),
        "space",
        scatter_dimension=0,
        tiled=True,
    )
    grad_weight = lax.psum(row_share, "frame").astype(jnp.float32) * grad_scale_factor
    grad_hidden = lax.dot_general(
        grad_rows, w_full, (((1,), (1,)), ((), ())), preferred_element_type=jnp.float32
    )
    grad_hidden = grad_hidden.reshape(values_in.shape)
    local_sums = jnp.stack(
        [jnp.sum(grad_hidden, axis=(1, 2, 3)), jnp.sum(grad_hidden * normed, axis=(1, 2, 3))],
        axis=1,
    )
    grad_modulation = lax.psum(local_sums, ("frame", "space")) * grad_scale_factor
    grad_normed = grad_hidden * (1.0 + scale)
    grad_input = (
        grad_normed
        - jnp.mean(grad_normed, axis=-1, keepdims=True)
        - normed * jnp.mean(grad_normed * normed, axis=-1, keepdims=True)
    ) * inverse_std
    return (grad_input.astype(jnp.bfloat16), grad_weight, grad_modulation)


def solution(mesh):
    in_specs = (
        P(None, "frame", "space", None, None),
        P(None, "frame", "space", None, None),
        P("space", None),
        P(),
        P(),
        P(),
        P(),
    )
    out_specs = (P(None, "frame", "space", None, None), P("space", None), P())
    return jax.shard_map(
        per_device, mesh=mesh, in_specs=in_specs, out_specs=out_specs, check_vma=False
    )
```

profile of v0, /device:TPU:2, one launch (start us, length us, event | category | flops | bytes accessed | tf_op | source)
XLA Modules:
  0.0 491.3 jit_solution(7075564899825200032)
XLA Ops:
  8.6 2.9 gather_fusion
  15.6 49.8 %all-gather.2.cloned.1.call-done = bf16[1152,3456]{1,0:T(8,128)(2,1)} async-done(((bf16[72,3456]{1,0:T(8,128)(2,1)}), bf16[1152,3456]{1,0:T(8,128)(2,1)}) %all-gather.2.cloned.1.call-update) | async-done | bytes 7962640 | tf_op jit(solution)/shard_map/all_gather | solution.py:48
  65.5 7.1 %convolution_convert_fusion.1 = bf16[256,3456]{1,0:T(8,128)(2,1)} fusion(bf16[256,1152]{1,0:T(8,128)(2,1)S(1)} %bitcast.76, bf16[1152,3456]{1,0:T(8,128)(2,1)} %all-gather.2.cloned.1.call-done), kind=kOutput, calls=%fused_computation.3 | convolution fusion | flops 2039316480 | bytes 10321920 | tf_op jit(solution)/shard_map/dot_general | solution.py:49
  72.6 2.6 copy.63
  75.2 2.0 reshape.124
  77.2 4.6 pad_maximum_fusion
  81.8 4.9 copy.66
  86.7 67.7 %all_to_all.8 = bf16[2,1,128,4,1152]{4,3,1,0,2:T(4,128)(2,1)S(1)} all-to-all(bf16[2,1,128,4,1152]{4,3,1,0,2:T(4,128)(2,1)} %copy.66), channel_id=1, replica_groups=mesh['frame'=16,'space'=16] {'frame'}, dimensions={2} | all-to-all | bytes 4718592 | tf_op jit(solution)/shard_map/all_to_all | solution.py:57
  154.4 8.8 %reshape.148 = bf16[2,16,8,4,16,72]{5,4,3,0,2,1:T(8,128)(2,1)} reshape(bf16[2,1,128,4,1152]{4,3,1,0,2:T(4,128)(2,1)S(1)} %all_to_all.8) | data formatting | bytes 4718592 | tf_op jit(solution)/shard_map/reshape | solution.py:61
  163.2 3.6 fusion.25
  166.8 1.7 fusion.1
  168.5 1.8 multiply_reduce_fusion
  170.2 2.4 fusion.9
  172.7 2.2 fusion.10
  174.9 3.0 fusion.8
  178.2 1.5 stack.21
  181.4 1.5 copy.75
  184.6 40.6 %all_to_all.9 = bf16[2,16,8,3,1152]{4,2,0,3,1:T(8,128)(2,1)S(1)} all-to-all(bf16[2,16,8,3,1152]{4,2,0,3,1:T(8,128)(2,1)S(1)} %copy.76), channel_id=1, replica_groups=mesh['frame'=16,'space'=16] {'frame'}, dimensions={1} | all-to-all | bytes 3538944 | tf_op jit(solution)/shard_map/all_to_all | solution.py:66
  227.2 5.5 %convolution_convert_fusion = bf16[1152,3456]{1,0:T(8,128)(2,1)} fusion(bf16[256,1152]{1,0:T(8,128)(2,1)S(1)} %bitcast.77, bf16[256,3456]{1,0:T(8,128)(2,1)S(1)} %bitcast.73), kind=kOutput, calls=%fused_computation.2 | convolution fusion | flops 2042413056 | bytes 10321920 | tf_op jit(solution)/shard_map/dot_general | solution.py:71
  232.8 6.5 %fusion.19 = (f32[256]{0:T(256)}, f32[256,1152]{1,0:T(8,128)S(1)}) fusion(f32[2,1152]{1,0:T(2,128)S(1)} %bitcast.80, bf16[256,3456]{1,0:T(8,128)(2,1)S(1)} %bitcast.74, bf16[1152,3456]{1,0:T(8,128)(2,1)} %all-gather.2.cloned.1.call-done), kind=kOutput, calls=%fused_computation.34 | convolution fusion | flops 2039021312 | bytes 10921984 | tf_op jit(solution)/shard_map/dot_general | solution.py:79
  240.6 77.9 %psum.15 = f32[2,2,1152]{2,0,1:T(2,128)S(1)} all-reduce(f32[2,2,1152]{2,0,1:T(2,128)S(1)} %pad_maximum_fusion.2), channel_id=1, replica_groups=mesh['frame'=16,'space'=16] {'frame','space'}, use_global_device_ids=true, to_apply=%region_10.0 | all-reduce | flops 4608 | bytes 36864 | tf_op jit(solution)/shard_map/psum | solution.py:87
  319.3 1.9 fusion.16
  321.2 161.5 %all-reduce.3.cloned.1.call-done = bf16[72,3456]{1,0:T(8,128)(2,1)} async-done(((bf16[72,3456]{1,0:T(8,128)(2,1)}), bf16[72,3456]{1,0:T(8,128)(2,1)}) %all-reduce.3.cloned.1.call-update) | async-done | bytes 497680 | tf_op jit(solution)/shard_map/psum | solution.py:78
  482.7 2.0 convert_multiply_fusion
  (58 shorter events, 13.1 us)
Async XLA Ops:
  7.2 5.1 %copy-start = (f32[1000]{0:T(1024)S(1)}, f32[1000]{0:T(1024)}, u32[]{:S(2)}) copy-start(f32[1000]{0:T(1024)} %param.11) | copy-start | bytes 12004
  7.2 7.6 %copy-start.2 = (bf16[2,1,2,64,1152]{4,3,2,1,0:T(8,128)(2,1)S(1)}, bf16[2,1,2,64,1152]{4,3,2,1,0:T(8,128)(2,1)}, u32[]{:S(2)}) copy-start(bf16[2,1,2,64,1152]{4,3,2,1,0:T(8,128)(2,1)} %param.7) | copy-start | bytes 1769476
  7.2 58.3 %all-gather.2.cloned.1.call-start = ((), (), s32[]{:S(2)}) async-start(), calls=%async_computation.3 | async-start | bytes 8460288 | tf_op jit(solution)/shard_map/all_gather | solution.py:48
  7.9 311.4 %reduce-scatter.5.cloned.1.call-start = ((), (), s32[]{:S(2)}) async-start(), calls=%async_computation.5 | async-start | bytes 8460288
  15.0 224.4 %copy-start.5 = (f32[2,2,64]{2,1,0:T(2,128)}, f32[2,2,64]{2,1,0:T(2,128)S(1)}, u32[]{:S(2)}) copy-start(f32[2,2,64]{2,1,0:T(2,128)S(1)} %broadcast_multiply_fusion.2) | copy-start | bytes 3076
  15.3 50.2 %copy-start.6 = (f32[2,2,64]{2,1,0:T(2,128)}, f32[2,2,64]{2,1,0:T(2,128)S(1)}, u32[]{:S(2)}) copy-start(f32[2,2,64]{2,1,0:T(2,128)S(1)} %add_rsqrt_fusion) | copy-start | bytes 3076
  15.6 49.8 %copy-start.3 = (bf16[2,1,2,64,1152]{4,3,2,1,0:T(8,128)(2,1)}, bf16[2,1,2,64,1152]{4,3,2,1,0:T(8,128)(2,1)S(1)}, u32[]{:S(2)}) copy-start(bf16[2,1,2,64,1152]{4,3,2,1,0:T(8,128)(2,1)S(1)} %fusion.12) | copy-start | bytes 1769476
  226.1 1.1 copy-start.4
  232.7 250.0 %all-reduce.3.cloned.1.call-start = ((), (), s32[]{:S(2)}) async-start(), calls=%async_computation.4 | async-start | bytes 995328 | tf_op jit(solution)/shard_map/psum | solution.py:78
  239.3 79.9 %copy-start.8 = (f32[256]{0:T(256)S(1)}, f32[256]{0:T(256)}, u32[]{:S(2)}) copy-start(f32[256]{0:T(256)} %get-tuple-element.25) | copy-start | bytes 3076
  239.4 79.9 %copy-start.7 = (f32[2,2,64]{2,1,0:T(2,128)S(1)}, f32[2,2,64]{2,1,0:T(2,128)}, u32[]{:S(2)}) copy-start(f32[2,2,64]{2,1,0:T(2,128)} %copy-done.6) | copy-start | bytes 3076
  319.3 165.5 %copy-start.1 = (f32[1000]{0:T(1024)S(1)}, f32[1000]{0:T(1024)}, u32[]{:S(2)}) copy-start(f32[1000]{0:T(1024)} %param.11) | copy-start | bytes 12004
Sparse Core Ops, SparseCore 0:
  9.9 55.5 all-gather.1
  232.9 74.6 reduce-scatter.4
  319.4 163.2 all-reduce.2
where the time goes:
time: 492 us; the launch traced here: 491 us
  waiting for transfers between devices  212 us (43%)
  blocking collectives  186 us (38%)
  local copies, waits for them, and re-layouts  35.1 us (7%)
  matrix products  30.3 us (6%)
  between operations  14 us (3%)
  other arithmetic  13.4 us (3%)
    psum x1, waiting for transfers between devices, per_device(): lax.psum(row_share, 'frame').astype(jnp.float32) * grad_scale_factor  162 us
    psum x1, blocking collectives, per_device(): lax.psum(local_sums, ('frame', 'space')) * grad_scale_factor  77.9 us
    all_to_all x1, blocking collectives, per_device(): lax.all_to_all(packed, 'frame', split_axis=2, concat_axis=1, tiled=True)  67.7 us
    all_gather x1, waiting for transfers between devices, per_device(): w_full = lax.all_gather(w_qkv, 'space', axis=0, tiled=True)  49.8 us
    all_to_all x1, blocking collectives, per_device(): lax.all_to_all(stacked, 'frame', split_axis=1, concat_axis=2, tiled=True)  40.6 us
  transfers between devices with their start and end apart: 3, of which 2 were waited for; matrix products, arithmetic and copies ran while one was open for 4% of the time, Pallas kernels for 0%

commit v1 on v0

--- a/solution.py
+++ b/solution.py
@@ -84,7 +84,7 @@
         [jnp.sum(grad_hidden, axis=(1, 2, 3)), jnp.sum(grad_hidden * normed, axis=(1, 2, 3))],
         axis=1,
     )
-    grad_modulation = lax.psum(local_sums, ("frame", "space")) * grad_scale_factor
+    grad_modulation = lax.psum(lax.psum(local_sums, "frame"), "space") * grad_scale_factor
     grad_normed = grad_hidden * (1.0 + scale)
     grad_input = (
         grad_normed

time: 492 us -> 545 us (1.11)
  blocking collectives: 186 us -> 239 us
    psum x1 -> x2, blocking collectives: 77.9 us -> 131 us  [the longest x1 81.5 us: per_device(): lax.psum(local_sums, 'frame')]
  transfers between devices with their start and end apart: 3 -> 3, of which waited for: 2 -> 2; matrix products, arithmetic and copies ran while one was open for 4% -> 3% of each run, Pallas kernels for 0% -> 0%
where the time goes in v1:
time: 545 us; the launch traced here: 544 us
  blocking collectives  239 us (44%)
  waiting for transfers between devices  212 us (39%)
  local copies, waits for them, and re-layouts  35.1 us (6%)
  matrix products  30.3 us (6%)
  between operations  14 us (3%)
  other arithmetic  13.4 us (2%)
    psum x1, waiting for transfers between devices, per_device(): lax.psum(row_share, 'frame').astype(jnp.float32) * grad_scale_factor  161 us
    psum x1, blocking collectives, per_device(): lax.psum(local_sums, 'frame')  81.5 us
    all_to_all x1, blocking collectives, per_device(): lax.all_to_all(packed, 'frame', split_axis=2, concat_axis=1, tiled=True)  67.7 us
    all_gather x1, waiting for transfers between devices, per_device(): w_full = lax.all_gather(w_qkv, 'space', axis=0, tiled=True)  49.8 us
    psum x1, blocking collectives, per_device(): lax.psum(lax.psum(local_sums, 'frame'), 'space') * grad_scale_factor  49.6 us
    all_to_all x1, blocking collectives, per_device(): lax.all_to_all(stacked, 'frame', split_axis=1, concat_axis=2, tiled=True)  40.6 us
  transfers between devices with their start and end apart: 3, of which 2 were waited for; matrix products, arithmetic and copies ran while one was open for 3% of the time, Pallas kernels for 0%

profile of v1, /device:TPU:2, one launch (start us, length us, event | category | flops | bytes accessed | tf_op | source)
XLA Modules:
  0.0 544.2 jit_solution(5557345247216517840)
XLA Ops:
  8.6 2.9 gather_fusion
  15.6 49.8 %all-gather.2.cloned.1.call-done = bf16[1152,3456]{1,0:T(8,128)(2,1)} async-done(((bf16[72,3456]{1,0:T(8,128)(2,1)}), bf16[1152,3456]{1,0:T(8,128)(2,1)}) %all-gather.2.cloned.1.call-update) | async-done | bytes 7962640 | tf_op jit(solution)/shard_map/all_gather | solution.py:48
  65.5 7.1 %convolution_convert_fusion.1 = bf16[256,3456]{1,0:T(8,128)(2,1)} fusion(bf16[256,1152]{1,0:T(8,128)(2,1)S(1)} %bitcast.76, bf16[1152,3456]{1,0:T(8,128)(2,1)} %all-gather.2.cloned.1.call-done), kind=kOutput, calls=%fused_computation.3 | convolution fusion | flops 2039316480 | bytes 10321920 | tf_op jit(solution)/shard_map/dot_general | solution.py:49
  72.6 2.6 copy.63
  75.2 2.0 reshape.124
  77.2 4.6 pad_maximum_fusion
  81.8 4.9 copy.66
  86.7 67.7 %all_to_all.8 = bf16[2,1,128,4,1152]{4,3,1,0,2:T(4,128)(2,1)S(1)} all-to-all(bf16[2,1,128,4,1152]{4,3,1,0,2:T(4,128)(2,1)} %copy.66), channel_id=1, replica_groups=mesh['frame'=16,'space'=16] {'frame'}, dimensions={2} | all-to-all | bytes 4718592 | tf_op jit(solution)/shard_map/all_to_all | solution.py:57
  154.4 8.8 %reshape.148 = bf16[2,16,8,4,16,72]{5,4,3,0,2,1:T(8,128)(2,1)} reshape(bf16[2,1,128,4,1152]{4,3,1,0,2:T(4,128)(2,1)S(1)} %all_to_all.8) | data formatting | bytes 4718592 | tf_op jit(solution)/shard_map/reshape | solution.py:61
  163.2 3.6 fusion.25
  166.8 1.7 fusion.1
  168.5 1.8 multiply_reduce_fusion
  170.2 2.4 fusion.9
  172.7 2.2 fusion.10
  174.9 3.0 fusion.8
  178.2 1.5 stack.21
  184.6 40.6 %all_to_all.9 = bf16[2,16,8,3,1152]{4,2,0,3,1:T(8,128)(2,1)S(1)} all-to-all(bf16[2,16,8,3,1152]{4,2,0,3,1:T(8,128)(2,1)S(1)} %copy.76), channel_id=1, replica_groups=mesh['frame'=16,'space'=16] {'frame'}, dimensions={1} | all-to-all | bytes 3538944 | tf_op jit(solution)/shard_map/all_to_all | solution.py:66
  227.2 5.5 %convolution_convert_fusion = bf16[1152,3456]{1,0:T(8,128)(2,1)} fusion(bf16[256,1152]{1,0:T(8,128)(2,1)S(1)} %bitcast.77, bf16[256,3456]{1,0:T(8,128)(2,1)S(1)} %bitcast.73), kind=kOutput, calls=%fused_computation.2 | convolution fusion | flops 2042413056 | bytes 10321920 | tf_op jit(solution)/shard_map/dot_general | solution.py:71
  232.8 6.5 %fusion.19 = (f32[256]{0:T(256)}, f32[256,1152]{1,0:T(8,128)S(1)}) fusion(f32[2,1152]{1,0:T(2,128)S(1)} %bitcast.80, bf16[256,3456]{1,0:T(8,128)(2,1)S(1)} %bitcast.74, bf16[1152,3456]{1,0:T(8,128)(2,1)} %all-gather.2.cloned.1.call-done), kind=kOutput, calls=%fused_computation.34 | convolution fusion | flops 2039021312 | bytes 10921984 | tf_op jit(solution)/shard_map/dot_general | solution.py:79
  240.6 81.5 %psum.22 = f32[2,2,1152]{2,0,1:T(2,128)S(1)} all-reduce(f32[2,2,1152]{2,0,1:T(2,128)S(1)} %pad_maximum_fusion.2), channel_id=1, replica_groups=mesh['frame'=16,'space'=16] {'frame'}, use_global_device_ids=true, to_apply=%region_10.0 | all-reduce | flops 4608 | bytes 36864 | tf_op jit(solution)/shard_map/psum | solution.py:87
  322.1 49.6 %psum.23 = f32[2,2,1152]{2,0,1:T(2,128)S(1)} all-reduce(f32[2,2,1152]{2,0,1:T(2,128)S(1)} %psum.22), channel_id=1, replica_groups=mesh['frame'=16,'space'=16] {'space'}, use_global_device_ids=true, to_apply=%region_11.0 | all-reduce | flops 4608 | bytes 36864 | tf_op jit(solution)/shard_map/psum | solution.py:87
  372.5 1.9 fusion.16
  374.4 161.3 %all-reduce.3.cloned.1.call-done = bf16[72,3456]{1,0:T(8,128)(2,1)} async-done(((bf16[72,3456]{1,0:T(8,128)(2,1)}), bf16[72,3456]{1,0:T(8,128)(2,1)}) %all-reduce.3.cloned.1.call-update) | async-done | bytes 497680 | tf_op jit(solution)/shard_map/psum | solution.py:78
  535.6 2.0 convert_multiply_fusion
  (59 shorter events, 14.6 us)
Async XLA Ops:
  7.2 5.1 copy-start
  7.2 7.6 %copy-start.2 = (bf16[2,1,2,64,1152]{4,3,2,1,0:T(8,128)(2,1)S(1)}, bf16[2,1,2,64,1152]{4,3,2,1,0:T(8,128)(2,1)}, u32[]{:S(2)}) copy-start(bf16[2,1,2,64,1152]{4,3,2,1,0:T(8,128)(2,1)} %param.7) | copy-start | bytes 1769476
  7.2 58.3 %all-gather.2.cloned.1.call-start = ((), (), s32[]{:S(2)}) async-start(), calls=%async_computation.3 | async-start | bytes 8460288 | tf_op jit(solution)/shard_map/all_gather | solution.py:48
  7.9 364.5 %reduce-scatter.5.cloned.1.call-start = ((), (), s32[]{:S(2)}) async-start(), calls=%async_computation.5 | async-start | bytes 8460288
  15.0 224.4 %copy-start.5 = (f32[2,2,64]{2,1,0:T(2,128)}, f32[2,2,64]{2,1,0:T(2,128)S(1)}, u32[]{:S(2)}) copy-start(f32[2,2,64]{2,1,0:T(2,128)S(1)} %broadcast_multiply_fusion.2) | copy-start | bytes 3076
  15.3 50.2 %copy-start.6 = (f32[2,2,64]{2,1,0:T(2,128)}, f32[2,2,64]{2,1,0:T(2,128)S(1)}, u32[]{:S(2)}) copy-start(f32[2,2,64]{2,1,0:T(2,128)S(1)} %add_rsqrt_fusion) | copy-start | bytes 3076
  15.6 49.8 %copy-start.3 = (bf16[2,1,2,64,1152]{4,3,2,1,0:T(8,128)(2,1)}, bf16[2,1,2,64,1152]{4,3,2,1,0:T(8,128)(2,1)S(1)}, u32[]{:S(2)}) copy-start(bf16[2,1,2,64,1152]{4,3,2,1,0:T(8,128)(2,1)S(1)} %fusion.12) | copy-start | bytes 1769476
  226.1 1.1 copy-start.4
  232.7 302.9 %all-reduce.3.cloned.1.call-start = ((), (), s32[]{:S(2)}) async-start(), calls=%async_computation.4 | async-start | bytes 995328 | tf_op jit(solution)/shard_map/psum | solution.py:78
  239.3 133.1 %copy-start.8 = (f32[256]{0:T(256)S(1)}, f32[256]{0:T(256)}, u32[]{:S(2)}) copy-start(f32[256]{0:T(256)} %get-tuple-element.25) | copy-start | bytes 3076
  239.4 133.1 %copy-start.7 = (f32[2,2,64]{2,1,0:T(2,128)S(1)}, f32[2,2,64]{2,1,0:T(2,128)}, u32[]{:S(2)}) copy-start(f32[2,2,64]{2,1,0:T(2,128)} %copy-done.6) | copy-start | bytes 3076
  372.4 165.2 %copy-start.1 = (f32[1000]{0:T(1024)S(1)}, f32[1000]{0:T(1024)}, u32[]{:S(2)}) copy-start(f32[1000]{0:T(1024)} %param.11) | copy-start | bytes 12004
Sparse Core Ops, SparseCore 0:
  9.9 55.5 all-gather.1
  232.9 75.3 reduce-scatter.4
  372.6 162.9 all-reduce.2
